TPU v7x, 128 devices: a whole 4x4x4 slice. The times are simulated.
128 devices in a mesh: row: 8 (over x, z_lo), col: 16 (over z_hi, y, core).
Axes of the slice: x: 4, y: 4, z: 4 (z_hi: 2, z_lo: 2; z = z_hi * 2 + z_lo), core: 2. Of those that a mesh axis runs over, the one named last changes fastest.
Arguments:
- factor_tiles: float32 [16, 1024, 8, 2048], P(None, 'row', None, 'col'), may hold values from -40 to 40, as said below
Outputs:
- rotated: float32 [16384, 16384], P(None, ('row', 'col'))
Inputs may be any that keep to these rules, and one draw needn't show every extreme that they name: `factor_tiles`: upper triangular: entries below the diagonal are zero, entries on it are positive.
All inputs are finite; a program needn't handle non-finite values.
Results may differ from a plain program's by a relative error of at most 0.0003.
Values sent between devices are 32-bit elements; how exact they have to be, the bound alone decides.
A program may use at most 128 MiB of HBM per device.

v0:
```python
import jax
import jax.numpy as jnp
from jax import lax
from jax.sharding import PartitionSpec as P

LOGB = 7
OUTER = 4
INNER = 8
damping_ratio = 0.01
highest = lax.Precision.HIGHEST


def passed_along(value, axis, steps):
    count = lax.axis_size(axis)
    leading, last = (max(0, -steps), min(count, count - steps))
    return lax.ppermute(value, axis, [(source, source + steps) for source in range(leading, last)])


def step_rotation(gram_matrix, stride):
    order = gram_matrix.shape[-1]
    index_row = jnp.arange(order)
    partner = jnp.bitwise_xor(index_row, stride)
    is_lead = jnp.bitwise_and(index_row, stride) == 0
    identity = index_row[:, None] == index_row[None, :]
    partner_mask = index_row[None, :] == partner[:, None]
    diagonal = jnp.sum(jnp.where(identity, gram_matrix, 0.0), axis=-1)
    diag_other = jnp.sum(jnp.where(partner_mask, diagonal[..., None, :], 0.0), axis=-1)
    cross_row = jnp.sum(jnp.where(partner_mask, gram_matrix, 0.0), axis=-1)
    cross_col = jnp.sum(jnp.where(partner_mask, gram_matrix, 0.0), axis=-2)
    diag_p = jnp.where(is_lead, diagonal, diag_other)
    diag_q = jnp.where(is_lead, diag_other, diagonal)
    cross = jnp.where(is_lead, cross_row, cross_col)
    diag_gap = diag_q - diag_p
    diag_sum = diag_p + diag_q
    rot_angle = 0.5 * jnp.arctan2(
        2.0 * cross * diag_gap, diag_gap * diag_gap + damping_ratio * diag_sum * diag_sum
    )
    cosine = jnp.cos(rot_angle)
    sine_val = jnp.where(is_lead, -jnp.sin(rot_angle), jnp.sin(rot_angle))
    turn = jnp.where(identity, cosine[..., None, :], 0.0)
    return turn + jnp.where(partner_mask, sine_val[..., None, :], 0.0)


def inner_solve(gram_matrix):
    order = gram_matrix.shape[-1]
    accum = jnp.eye(order, dtype=gram_matrix.dtype)
    for inner_step in range(INNER):
        bit_index = (LOGB - 1 - inner_step) % LOGB
        turn = step_rotation(gram_matrix, 2**bit_index)
        gram_matrix = jnp.einsum("...ik,...kj->...ij", gram_matrix, turn, precision=highest)
        gram_matrix = jnp.einsum("...ki,...kj->...ij", turn, gram_matrix, precision=highest)
        accum = jnp.einsum("...ik,...kj->...ij", accum, turn, precision=highest)
    return accum


def relayout(tile_work):
    cycles, row_count, tile_count, tile_width = tile_work.shape
    split_view = tile_work.reshape(cycles, 1, row_count, tile_count, tile_width)
    received = lax.all_to_all(split_view, "row", split_axis=3, concat_axis=1, tiled=True)
    return received.reshape(cycles * received.shape[1] * row_count, tile_width)


def per_device(factor_tiles):
    half_width = factor_tiles.shape[-1] // 2
    column_block = relayout(factor_tiles)
    position = lax.axis_index(("row", "col"))
    devices_total = lax.axis_size(("row", "col"))
    gram_matrix = jnp.einsum("ni,nj->ij", column_block, column_block, precision=highest)
    rotation = inner_solve(gram_matrix)
    block_lines = jnp.einsum("ni,ij->jn", column_block, rotation, precision=highest)
    for round_index in range(1, OUTER):
        top_half = block_lines[:half_width]
        bottom_half = block_lines[half_width:]
        outgoing = jnp.where(position == 0, bottom_half, top_half)
        arrived = passed_along(outgoing, ("row", "col"), 1)
        behind = passed_along(bottom_half, ("row", "col"), -1)
        new_top = jnp.where(position == 0, top_half, arrived)
        new_bottom = jnp.where(position == devices_total - 1, top_half, behind)
        block_lines = jnp.concatenate([new_top, new_bottom], axis=0)
        gram_matrix = jnp.einsum("in,jn->ij", block_lines, block_lines, precision=highest)
        rotation = inner_solve(gram_matrix)
        if round_index + 1 < OUTER:
            block_lines = jnp.einsum("in,ij->jn", block_lines, rotation, precision=highest)
        else:
            return jnp.einsum("in,ij->nj", block_lines, rotation, precision=highest)


def solution(mesh):
    return jax.shard_map(
        per_device,
        mesh=mesh,
        in_specs=(P(None, "row", None, "col"),),
        out_specs=P(None, ("row", "col")),
        check_vma=False,
    )
```

profile of v0, /device:TPU:25, one launch (start us, length us, event | category | flops | bytes accessed | tf_op | source)
XLA Modules:
  0.0 464.9 jit_solution(8180532006522970439)
XLA Ops:
  0.0 9.3 %copy.7 = f32[16,128,8,128]{1,3,0,2:T(8,128)} copy(f32[16,128,8,128]{3,2,1,0:T(8,128)} %param.1) | data formatting | bytes 16777216 | tf_op args[0]
  9.3 5.4 %all-to-all-start = ((f32[16,1,128,8,128]{2,4,0,1,3:T(8,128)}), f32[16,1,128,8,128]{2,4,0,1,3:T(8,128)}, u32[]{:S(2)}, u32[]{:S(2)}) async-start(f32[16,1,128,8,128]{2,4,0,1,3:T(8,128)} %bitcast.113), calls=%async_computation | async-start | bytes 16777216 | tf_op jit(solution)/shard_map/all_to_all | solution.py:59
  14.7 115.1 %all-to-all-done = f32[16,1,128,8,128]{2,4,0,1,3:T(8,128)} async-done(((f32[16,1,128,8,128]{2,4,0,1,3:T(8,128)}), f32[16,1,128,8,128]{2,4,0,1,3:T(8,128)}, u32[]{:S(2)}, u32[]{:S(2)}) %all-to-all-start) | async-done | bytes 8388640 | tf_op jit(solution)/shard_map/all_to_all | solution.py:59
  129.7 7.9 %copy.30 = f32[16,1,128,8,128]{2,4,3,0,1:T(8,128)} copy(f32[16,1,128,8,128]{2,4,0,1,3:T(8,128)} %all-to-all-done) | data formatting | bytes 16777216 | tf_op jit(solution)/shard_map/all_to_all | solution.py:59
  137.6 9.3 %copy.10 = f32[16,8,1,128,1,128]{5,3,1,0,4,2:T(8,128)} copy(f32[16,8,1,128,1,128]{3,5,1,0,4,2:T(8,128)} %bitcast.114) | data formatting | bytes 16777216 | tf_op jit(solution)/shard_map/all_to_all | solution.py:59
  146.9 10.9 %fusion.152 = (f32[128]{0:T(128)S(1)}, f32[128]{0:T(128)S(1)}, f32[128]{0:T(128)S(1)}, f32[128,128]{0,1:T(8,128)S(1)}) fusion(s32[128]{0:T(128)S(1)} %iota_xor_fusion.6, f32[16,1,128,8,128]{2,4,0,1,3:T(8,128)} %all-to-all-done), kind=kOutput, calls=%fused_computation.257 | convolution fusion | flops 3221339648 | bytes 8456192 | tf_op jit(solution)/shard_map/ni,nj->ij/dot_general | solution.py:68
  167.8 9.3 %fusion.822 = f32[128,16384]{1,0:T(8,128)S(1)} fusion(f32[128,128]{1,0:T(8,128)S(1)} %fusion.90, f32[16384,128]{1,0:T(8,128)S(1)} %bitcast.112), kind=kOutput, calls=%fused_computation.973 | convolution fusion | flops 3221225472 | bytes 16842752 | tf_op jit(solution)/shard_map/ni,ij->jn/dot_general | solution.py:70
  177.1 4.1 slice_select_fusion.8
  181.2 1.8 copy-done
  183.0 6.4 %collective-permute-start = (f32[64,16384]{1,0:T(8,128)}, f32[64,16384]{1,0:T(8,128)}, u32[]{:S(2)}, u32[]{:S(2)}) collective-permute-start(f32[64,16384]{1,0:T(8,128)} %get-tuple-element.175), channel_id=1, source_target_pairs={{0,1},{1,2},{2,3},{3,4},{4,5},{5,6},{6,7},{7,8},{8,9},{9,10},{10,1... | collective-permute-start | bytes 12582920 | tf_op jit(solution)/shard_map/ppermute | solution.py:16
  189.4 1.9 collective-permute-start.1
  191.3 43.8 %collective-permute-done = f32[64,16384]{1,0:T(8,128)} collective-permute-done((f32[64,16384]{1,0:T(8,128)}, f32[64,16384]{1,0:T(8,128)}, u32[]{:S(2)}, u32[]{:S(2)}) %collective-permute-start) | collective-permute-done | bytes 4194336 | tf_op jit(solution)/shard_map/ppermute | solution.py:16
  235.1 8.0 %collective-permute-done.1 = f32[64,16384]{1,0:T(8,128)} collective-permute-done((f32[64,16384]{1,0:T(8,128)}, f32[64,16384]{1,0:T(8,128)}, u32[]{:S(2)}, u32[]{:S(2)}) %collective-permute-start.1) | collective-permute-done | bytes 4194336 | tf_op jit(solution)/shard_map/ppermute | solution.py:16
  243.1 5.3 %slice_select_fusion.7 = (f32[64,16384]{1,0:T(8,128)S(1)}, f32[64,16384]{1,0:T(8,128)S(1)}) fusion(f32[64,16384]{1,0:T(8,128)} %collective-permute-done, f32[128,16384]{1,0:T(8,128)} %copy-done, pred[]{:T(512)S(6)} %eq.1664, f32[64,16384]{1,0:T(8,128)} %collective-permute-done.1, pred[]{:T(512)S(6)} %eq.1694), kind=kLoop, calls=%fused_computation.21 | loop fusion | flops 2097152 | bytes 20971522 | tf_op jit(solution)/shard_map/jit(_where)/select_n | solution.py:77
  248.5 6.7 %fusion.156 = (f32[128]{0:T(128)S(1)}, f32[128]{0:T(128)S(1)}, f32[128]{0:T(128)S(1)}, f32[128,128]{0,1:T(8,128)S(1)}) fusion(s32[128]{0:T(128)S(1)} %iota_xor_fusion.6, f32[64,16384]{1,0:T(8,128)S(1)} %get-tuple-element.174, f32[64,16384]{1,0:T(8,128)S(1)} %get-tuple-element.173), kind=kOutput, calls=%fused_computation.261 | convolution fusion | flops 3223436800 | bytes 8456192 | tf_op jit(solution)/shard_map/in,jn->ij/dot_general | solution.py:80
  265.4 7.7 %fusion.8 = f32[128,16384]{1,0:T(8,128)S(1)} fusion(f32[128,128]{1,0:T(8,128)S(1)} %fusion.65, f32[64,16384]{1,0:T(8,128)S(1)} %copy-done.3, f32[64,16384]{1,0:T(8,128)S(1)} %get-tuple-element.173), kind=kOutput, calls=%fused_computation.12 | convolution fusion | flops 3223322624 | bytes 16842752 | tf_op jit(solution)/shard_map/in,ij->jn/dot_general | solution.py:83
  273.8 1.9 collective-permute-start.2
  275.7 2.8 collective-permute-start.3
  278.5 42.6 %collective-permute-done.2 = f32[64,16384]{1,0:T(8,128)S(1)} collective-permute-done((f32[64,16384]{1,0:T(8,128)S(1)}, f32[64,16384]{1,0:T(8,128)S(1)}, u32[]{:S(2)}, u32[]{:S(2)}) %collective-permute-start.2) | collective-permute-done | bytes 4194336 | tf_op jit(solution)/shard_map/ppermute | solution.py:16
  321.1 2.0 copy-done.8
  323.2 6.1 %collective-permute-done.3 = f32[64,16384]{1,0:T(8,128)} collective-permute-done((f32[64,16384]{1,0:T(8,128)S(1)}, f32[64,16384]{1,0:T(8,128)}, u32[]{:S(2)}, u32[]{:S(2)}) %collective-permute-start.3) | collective-permute-done | bytes 4194336 | tf_op jit(solution)/shard_map/ppermute | solution.py:16
  329.3 6.2 %slice_select_fusion.4 = (f32[64,16384]{1,0:T(8,128)S(1)}, f32[64,16384]{1,0:T(8,128)}) fusion(f32[64,16384]{1,0:T(8,128)} %copy-done.8, f32[128,16384]{1,0:T(8,128)S(1)} %fusion.8, pred[]{:T(512)S(6)} %eq.1664, f32[64,16384]{1,0:T(8,128)} %collective-permute-done.3, pred[]{:T(512)S(6)} %eq.1694), kind=kLoop, calls=%fused_computation.18 | loop fusion | flops 2097152 | bytes 20971522 | tf_op jit(solution)/shard_map/jit(_where)/select_n | solution.py:77
  335.4 11.7 %fusion.160 = (f32[128]{0:T(128)S(1)}, f32[128]{0:T(128)S(1)}, f32[128]{0:T(128)S(1)}, f32[128,128]{0,1:T(8,128)S(1)}) fusion(s32[128]{0:T(128)S(1)} %iota_xor_fusion.6, f32[64,16384]{1,0:T(8,128)} %get-tuple-element.170, f32[64,16384]{1,0:T(8,128)S(1)} %get-tuple-element.169), kind=kOutput, calls=%fused_computation.265 | convolution fusion | flops 3223436800 | bytes 8456192 | tf_op jit(solution)/shard_map/in,jn->ij/dot_general | solution.py:80
  357.3 9.2 %fusion.6 = f32[128,16384]{1,0:T(8,128)S(1)} fusion(f32[128,128]{1,0:T(8,128)S(1)} %fusion.40, f32[64,16384]{1,0:T(8,128)} %get-tuple-element.170, f32[64,16384]{1,0:T(8,128)S(1)} %copy-done.5), kind=kOutput, calls=%fused_computation.10 | convolution fusion | flops 3223322624 | bytes 16842752 | tf_op jit(solution)/shard_map/in,ij->jn/dot_general | solution.py:83
  367.2 1.9 collective-permute-start.4
  369.2 2.4 collective-permute-start.5
  371.6 43.0 %collective-permute-done.4 = f32[64,16384]{1,0:T(8,128)S(1)} collective-permute-done((f32[64,16384]{1,0:T(8,128)S(1)}, f32[64,16384]{1,0:T(8,128)S(1)}, u32[]{:S(2)}, u32[]{:S(2)}) %collective-permute-start.4) | collective-permute-done | bytes 4194336 | tf_op jit(solution)/shard_map/ppermute | solution.py:16
  414.6 2.0 copy-done.7
  416.6 6.1 %collective-permute-done.5 = f32[64,16384]{1,0:T(8,128)} collective-permute-done((f32[64,16384]{1,0:T(8,128)S(1)}, f32[64,16384]{1,0:T(8,128)}, u32[]{:S(2)}, u32[]{:S(2)}) %collective-permute-start.5) | collective-permute-done | bytes 4194336 | tf_op jit(solution)/shard_map/ppermute | solution.py:16
  422.7 6.2 %slice_select_fusion.1 = (f32[64,16384]{1,0:T(8,128)S(1)}, f32[64,16384]{1,0:T(8,128)}) fusion(f32[64,16384]{1,0:T(8,128)} %copy-done.7, f32[128,16384]{1,0:T(8,128)S(1)} %fusion.6, pred[]{:T(512)S(6)} %eq.1664, f32[64,16384]{1,0:T(8,128)} %collective-permute-done.5, pred[]{:T(512)S(6)} %eq.1694), kind=kLoop, calls=%fused_computation.15 | loop fusion | flops 2097152 | bytes 20971522 | tf_op jit(solution)/shard_map/jit(_where)/select_n | solution.py:77
  428.9 10.2 %fusion.164 = (f32[128]{0:T(128)S(1)}, f32[128]{0:T(128)S(1)}, f32[128]{0:T(128)S(1)}, f32[128,128]{0,1:T(8,128)S(1)}) fusion(s32[128]{0:T(128)S(1)} %iota_xor_fusion.6, f32[64,16384]{1,0:T(8,128)} %get-tuple-element.166, f32[64,16384]{1,0:T(8,128)S(1)} %get-tuple-element.165), kind=kOutput, calls=%fused_computation.269 | convolution fusion | flops 3223436800 | bytes 8456192 | tf_op jit(solution)/shard_map/in,jn->ij/dot_general | solution.py:80
  449.3 15.4 %fusion.4 = f32[16384,128]{1,0:T(8,128)} fusion(f32[128,128]{1,0:T(8,128)S(1)} %fusion.15, f32[64,16384]{1,0:T(8,128)S(1)} %copy-done.1, f32[64,16384]{1,0:T(8,128)S(1)} %get-tuple-element.165), kind=kOutput, calls=%fused_computation.8 | convolution fusion | flops 3223322624 | bytes 16842752 | tf_op jit(solution)/shard_map/in,ij->nj/dot_general | solution.py:85
  (205 shorter events, 41.3 us)
Async XLA Ops:
  9.3 120.5 %all-to-all-start = ((f32[16,1,128,8,128]{2,4,0,1,3:T(8,128)}), f32[16,1,128,8,128]{2,4,0,1,3:T(8,128)}, u32[]{:S(2)}, u32[]{:S(2)}) async-start(f32[16,1,128,8,128]{2,4,0,1,3:T(8,128)} %bitcast.113), calls=%async_computation | async-start | bytes 16777216 | tf_op jit(solution)/shard_map/all_to_all | solution.py:59
  146.9 20.9 %copy-start.6 = (f32[16,8,1,128,1,128]{5,3,1,0,4,2:T(8,128)S(1)}, f32[16,8,1,128,1,128]{5,3,1,0,4,2:T(8,128)}, u32[]{:S(2)}) copy-start(f32[16,8,1,128,1,128]{5,3,1,0,4,2:T(8,128)} %copy.10) | copy-start | bytes 25165828
  177.1 5.9 %copy-start = (f32[128,16384]{1,0:T(8,128)}, f32[128,16384]{1,0:T(8,128)S(1)}, u32[]{:S(2)}) copy-start(f32[128,16384]{1,0:T(8,128)S(1)} %fusion.822) | copy-start | bytes 25165828
  183.0 52.1 %collective-permute-start = (f32[64,16384]{1,0:T(8,128)}, f32[64,16384]{1,0:T(8,128)}, u32[]{:S(2)}, u32[]{:S(2)}) collective-permute-start(f32[64,16384]{1,0:T(8,128)} %get-tuple-element.175), channel_id=1, source_target_pairs={{0,1},{1,2},{2,3},{3,4},{4,5},{5,6},{6,7},{7,8},{8,9},{9,10},{10,1... | collective-permute-start | bytes 12582920 | tf_op jit(solution)/shard_map/ppermute | solution.py:16
  189.4 53.8 %collective-permute-start.1 = (f32[64,16384]{1,0:T(8,128)}, f32[64,16384]{1,0:T(8,128)}, u32[]{:S(2)}, u32[]{:S(2)}) collective-permute-start(f32[64,16384]{1,0:T(8,128)} %get-tuple-element.176), channel_id=1, source_target_pairs={{1,0},{2,1},{3,2},{4,3},{5,4},{6,5},{7,6},{8,7},{9,8},{10,9},{11,1... | collective-permute-start | bytes 12582920 | tf_op jit(solution)/shard_map/ppermute | solution.py:16
  248.5 6.7 %copy-start.2 = (f32[64,16384]{1,0:T(8,128)}, f32[64,16384]{1,0:T(8,128)S(1)}, u32[]{:S(2)}) copy-start(f32[64,16384]{1,0:T(8,128)S(1)} %get-tuple-element.174) | copy-start | bytes 12582916
  255.2 10.2 %copy-start.3 = (f32[64,16384]{1,0:T(8,128)S(1)}, f32[64,16384]{1,0:T(8,128)}, u32[]{:S(2)}) copy-start(f32[64,16384]{1,0:T(8,128)} %copy-done.2) | copy-start | bytes 12582916
  273.8 47.4 %collective-permute-start.2 = (f32[64,16384]{1,0:T(8,128)S(1)}, f32[64,16384]{1,0:T(8,128)S(1)}, u32[]{:S(2)}, u32[]{:S(2)}) collective-permute-start(f32[64,16384]{1,0:T(8,128)S(1)} %get-tuple-element.171), channel_id=1, source_target_pairs={{0,1},{1,2},{2,3},{3,4},{4,5},{5,6},{6,7},{7,8},{8,9},{9,10},{10,1... | collective-permute-start | bytes 12582920 | tf_op jit(solution)/shard_map/ppermute | solution.py:16
  275.7 53.5 %collective-permute-start.3 = (f32[64,16384]{1,0:T(8,128)S(1)}, f32[64,16384]{1,0:T(8,128)}, u32[]{:S(2)}, u32[]{:S(2)}) collective-permute-start(f32[64,16384]{1,0:T(8,128)S(1)} %get-tuple-element.172), channel_id=1, source_target_pairs={{1,0},{2,1},{3,2},{4,3},{5,4},{6,5},{7,6},{8,7},{9,8},{10,9},{11,1... | collective-permute-start | bytes 12582920 | tf_op jit(solution)/shard_map/ppermute | solution.py:16
  321.1 2.0 copy-start.8
  335.4 11.7 %copy-start.4 = (f32[64,16384]{1,0:T(8,128)}, f32[64,16384]{1,0:T(8,128)S(1)}, u32[]{:S(2)}) copy-start(f32[64,16384]{1,0:T(8,128)S(1)} %get-tuple-element.169) | copy-start | bytes 12582916
  347.1 10.2 %copy-start.5 = (f32[64,16384]{1,0:T(8,128)S(1)}, f32[64,16384]{1,0:T(8,128)}, u32[]{:S(2)}) copy-start(f32[64,16384]{1,0:T(8,128)} %copy-done.4) | copy-start | bytes 12582916
  367.2 47.4 %collective-permute-start.4 = (f32[64,16384]{1,0:T(8,128)S(1)}, f32[64,16384]{1,0:T(8,128)S(1)}, u32[]{:S(2)}, u32[]{:S(2)}) collective-permute-start(f32[64,16384]{1,0:T(8,128)S(1)} %get-tuple-element.167), channel_id=1, source_target_pairs={{0,1},{1,2},{2,3},{3,4},{4,5},{5,6},{6,7},{7,8},{8,9},{9,10},{10,1... | collective-permute-start | bytes 12582920 | tf_op jit(solution)/shard_map/ppermute | solution.py:16
  369.2 53.5 %collective-permute-start.5 = (f32[64,16384]{1,0:T(8,128)S(1)}, f32[64,16384]{1,0:T(8,128)}, u32[]{:S(2)}, u32[]{:S(2)}) collective-permute-start(f32[64,16384]{1,0:T(8,128)S(1)} %get-tuple-element.168), channel_id=1, source_target_pairs={{1,0},{2,1},{3,2},{4,3},{5,4},{6,5},{7,6},{8,7},{9,8},{10,9},{11,1... | collective-permute-start | bytes 12582920 | tf_op jit(solution)/shard_map/ppermute | solution.py:16
  414.6 2.0 copy-start.7
  439.1 10.2 %copy-start.1 = (f32[64,16384]{1,0:T(8,128)S(1)}, f32[64,16384]{1,0:T(8,128)}, u32[]{:S(2)}) copy-start(f32[64,16384]{1,0:T(8,128)} %get-tuple-element.166) | copy-start | bytes 12582916
where the time goes:
time: 470 us; the launch traced here: 465 us
  waiting for transfers between devices  265 us (56%)
  matrix products  114 us (24%)
  local copies, waits for them, and re-layouts  32.3 us (7%)
  other arithmetic  30.5 us (6%)
  starting transfers between devices  22.7 us (5%)
    ppermute x6, waiting for transfers between devices, passed_along(): lax.ppermute(value, axis, [(source, source + steps) for source in range(l...  150 us
    all_to_all x1, waiting for transfers between devices, relayout(): lax.all_to_all(split_view, 'row', split_axis=3, concat_axis=1, tiled=True)  115 us
    dot_general x3, matrix products, per_device(): jnp.einsum('in,jn->ij', block_lines, block_lines, precision=highest)  28.6 us
    select_n x3, other arithmetic, per_device(): new_top = jnp.where(position == 0, top_half, arrived)  17.7 us
    ppermute x6, starting transfers between devices, passed_along(): lax.ppermute(value, axis, [(source, source + steps) for source in range(l...  17.4 us
    all_to_all x2, local copies, waits for them, and re-layouts, relayout(): lax.all_to_all(split_view, 'row', split_axis=3, concat_axis=1, tiled=True)  17.2 us
    dot_general x2, matrix products, per_device(): jnp.einsum('in,ij->jn', block_lines, rotation, precision=highest)  16.9 us
    dot_general x1, matrix products, per_device(): return jnp.einsum('in,ij->nj', block_lines, rotation, precision=highest)  15.4 us
  transfers between devices with their start and end apart: 7, of which 7 were waited for; matrix products, arithmetic and copies ran while one was open for 0% of the time, Pallas kernels for 0%

commit v1 on v0

--- a/solution.py
+++ b/solution.py
@@ -2,6 +2,7 @@
 import jax.numpy as jnp
 from jax import lax
 from jax.sharding import PartitionSpec as P
+from jax.lax import all_to_all, axis_size
 
 LOGB = 7
 OUTER = 4
@@ -56,7 +57,9 @@
 def relayout(tile_work):
     cycles, row_count, tile_count, tile_width = tile_work.shape
     split_view = tile_work.reshape(cycles, 1, row_count, tile_count, tile_width)
-    received = lax.all_to_all(split_view, "row", split_axis=3, concat_axis=1, tiled=True)
+    received = jnp.concatenate(
+        all_to_all(jnp.stack(jnp.split(split_view, axis_size("row"), axis=3)), "row", 0, 0), axis=1
+    )
     return received.reshape(cycles * received.shape[1] * row_count, tile_width)
 
 

time: 470 us -> 485 us (1.032)
  local copies, waits for them, and re-layouts: 32.3 us -> 46.6 us
    unnamed x19 -> x22, local copies, waits for them, and re-layouts: 15.1 us -> 28.4 us
    all_to_all x2 -> x1, local copies, waits for them, and re-layouts: 17.2 us -> 7.89 us  [relayout(): all_to_all(jnp.stack(jnp.split(split_view, axis_size('row'), axis=3)), 'r...]
    reshape x0 -> x1, local copies, waits for them, and re-layouts: none -> 9.26 us  [relayout(): jnp.concatenate(all_to_all(jnp.stack(jnp.split(split_view, axis_size('row...]
where the time goes in v1:
time: 485 us; the launch traced here: 480 us
  waiting for transfers between devices  265 us (55%)
  matrix products  114 us (24%)
  local copies, waits for them, and re-layouts  46.6 us (10%)
  other arithmetic  30.6 us (6%)
  starting transfers between devices  22.5 us (5%)
    ppermute x6, waiting for transfers between devices, passed_along(): lax.ppermute(value, axis, [(source, source + steps) for source in range(l...  150 us
    all_to_all x1, waiting for transfers between devices, relayout(): all_to_all(jnp.stack(jnp.split(split_view, axis_size('row'), axis=3)), 'r...  115 us
    unnamed x22, local copies, waits for them, and re-layouts  28.4 us
    dot_general x3, matrix products, per_device(): jnp.einsum('in,jn->ij', block_lines, block_lines, precision=highest)  27.3 us
    dot_general x2, matrix products, per_device(): jnp.einsum('in,ij->jn', block_lines, rotation, precision=highest)  18.3 us
    select_n x3, other arithmetic, per_device(): new_top = jnp.where(position == 0, top_half, arrived)  17.7 us
    ppermute x6, starting transfers between devices, passed_along(): lax.ppermute(value, axis, [(source, source + steps) for source in range(l...  17.1 us
    dot_general x1, matrix products, per_device(): return jnp.einsum('in,ij->nj', block_lines, rotation, precision=highest)  15.4 us
  transfers between devices with their start and end apart: 7, of which 7 were waited for; matrix products, arithmetic and copies ran while one was open for 0% of the time, Pallas kernels for 0%

profile of v1, /device:TPU:25, one launch (start us, length us, event | category | flops | bytes accessed | tf_op | source)
XLA Modules:
  0.0 479.6 jit_solution(9435263857929486354)
XLA Ops:
  0.0 9.3 %copy.21 = f32[16,128,8,128]{1,3,0,2:T(8,128)} copy(f32[16,128,8,128]{3,2,1,0:T(8,128)} %param.1) | data formatting | bytes 16777216 | tf_op args[0]
  9.3 2.5 fusion.22
  11.8 2.8 fusion.21
  14.6 2.3 fusion.20
  16.9 2.3 fusion.19
  23.6 5.4 %all-to-all-start = ((f32[8,16,1,128,1,128]{3,5,1,4,2,0:T(8,128)}), f32[8,16,1,128,1,128]{3,5,1,4,2,0:T(8,128)}, u32[]{:S(2)}, u32[]{:S(2)}) async-start(f32[8,16,1,128,1,128]{3,5,1,4,2,0:T(8,128)} %fusion.15), calls=%async_computation | async-start | bytes 16777216 | tf_op jit(solution)/shard_map/all_to_all | solution.py:61
  29.0 115.1 %all-to-all-done = f32[8,16,1,128,1,128]{3,5,1,4,2,0:T(8,128)} async-done(((f32[8,16,1,128,1,128]{3,5,1,4,2,0:T(8,128)}), f32[8,16,1,128,1,128]{3,5,1,4,2,0:T(8,128)}, u32[]{:S(2)}, u32[]{:S(2)}) %all-to-all-start) | async-done | bytes 8388640 | tf_op jit(solution)/shard_map/all_to_all | solution.py:61
  144.1 7.9 %copy.44 = f32[8,16,1,128,1,128]{3,5,0,1,4,2:T(8,128)} copy(f32[8,16,1,128,1,128]{3,5,1,4,2,0:T(8,128)} %all-to-all-done) | data formatting | bytes 16777216 | tf_op jit(solution)/shard_map/all_to_all | solution.py:61
  152.0 9.3 %copy.24 = f32[16,8,1,128,1,128]{5,3,1,0,4,2:T(8,128)} copy(f32[16,8,1,128,1,128]{3,5,1,0,4,2:T(8,128)} %bitcast.151) | data formatting | bytes 16777216 | tf_op jit(solution)/shard_map/reshape | solution.py:60
  161.3 10.9 %fusion.160 = (f32[128]{0:T(128)S(1)}, f32[128]{0:T(128)S(1)}, f32[128]{0:T(128)S(1)}, f32[128,128]{0,1:T(8,128)S(1)}) fusion(s32[128]{0:T(128)S(1)} %iota_xor_fusion.6, f32[8,16,1,128,1,128]{3,5,1,4,2,0:T(8,128)} %all-to-all-done), kind=kOutput, calls=%fused_computation.273 | convolution fusion | flops 3221339648 | bytes 8456192 | tf_op jit(solution)/shard_map/ni,nj->ij/dot_general | solution.py:71
  182.1 9.3 %fusion.830 = f32[128,16384]{1,0:T(8,128)S(1)} fusion(f32[128,128]{1,0:T(8,128)S(1)} %fusion.98, f32[16384,128]{1,0:T(8,128)S(1)} %bitcast.150), kind=kOutput, calls=%fused_computation.989 | convolution fusion | flops 3221225472 | bytes 16842752 | tf_op jit(solution)/shard_map/ni,ij->jn/dot_general | solution.py:73
  191.5 4.1 slice_select_fusion.8
  197.4 6.4 %collective-permute-start = (f32[64,16384]{1,0:T(8,128)}, f32[64,16384]{1,0:T(8,128)}, u32[]{:S(2)}, u32[]{:S(2)}) collective-permute-start(f32[64,16384]{1,0:T(8,128)} %get-tuple-element.175), channel_id=1, source_target_pairs={{0,1},{1,2},{2,3},{3,4},{4,5},{5,6},{6,7},{7,8},{8,9},{9,10},{10,1... | collective-permute-start | bytes 12582920 | tf_op jit(solution)/shard_map/ppermute | solution.py:17
  205.7 43.8 %collective-permute-done = f32[64,16384]{1,0:T(8,128)} collective-permute-done((f32[64,16384]{1,0:T(8,128)}, f32[64,16384]{1,0:T(8,128)}, u32[]{:S(2)}, u32[]{:S(2)}) %collective-permute-start) | collective-permute-done | bytes 4194336 | tf_op jit(solution)/shard_map/ppermute | solution.py:17
  249.5 8.0 %collective-permute-done.1 = f32[64,16384]{1,0:T(8,128)} collective-permute-done((f32[64,16384]{1,0:T(8,128)}, f32[64,16384]{1,0:T(8,128)}, u32[]{:S(2)}, u32[]{:S(2)}) %collective-permute-start.1) | collective-permute-done | bytes 4194336 | tf_op jit(solution)/shard_map/ppermute | solution.py:17
  257.5 5.3 %slice_select_fusion.7 = (f32[64,16384]{1,0:T(8,128)S(1)}, f32[64,16384]{1,0:T(8,128)S(1)}) fusion(f32[64,16384]{1,0:T(8,128)} %collective-permute-done, f32[128,16384]{1,0:T(8,128)} %copy-done, pred[]{:T(512)S(6)} %eq.1664, f32[64,16384]{1,0:T(8,128)} %collective-permute-done.1, pred[]{:T(512)S(6)} %eq.1694), kind=kLoop, calls=%fused_computation.21 | loop fusion | flops 2097152 | bytes 20971522 | tf_op jit(solution)/shard_map/jit(_where)/select_n | solution.py:80
  262.8 6.7 %fusion.164 = (f32[128]{0:T(128)S(1)}, f32[128]{0:T(128)S(1)}, f32[128]{0:T(128)S(1)}, f32[128,128]{0,1:T(8,128)S(1)}) fusion(s32[128]{0:T(128)S(1)} %iota_xor_fusion.6, f32[64,16384]{1,0:T(8,128)S(1)} %get-tuple-element.174, f32[64,16384]{1,0:T(8,128)S(1)} %get-tuple-element.173), kind=kOutput, calls=%fused_computation.277 | convolution fusion | flops 3223436800 | bytes 8456192 | tf_op jit(solution)/shard_map/in,jn->ij/dot_general | solution.py:83
  279.7 9.2 %fusion.8 = f32[128,16384]{1,0:T(8,128)S(1)} fusion(f32[128,128]{1,0:T(8,128)S(1)} %fusion.73, f32[64,16384]{1,0:T(8,128)} %copy-done.2, f32[64,16384]{1,0:T(8,128)S(1)} %get-tuple-element.173), kind=kOutput, calls=%fused_computation.12 | convolution fusion | flops 3223322624 | bytes 16842752 | tf_op jit(solution)/shard_map/in,ij->jn/dot_general | solution.py:86
  291.6 2.4 collective-permute-start.3
  294.0 43.0 %collective-permute-done.2 = f32[64,16384]{1,0:T(8,128)S(1)} collective-permute-done((f32[64,16384]{1,0:T(8,128)S(1)}, f32[64,16384]{1,0:T(8,128)S(1)}, u32[]{:S(2)}, u32[]{:S(2)}) %collective-permute-start.2) | collective-permute-done | bytes 4194336 | tf_op jit(solution)/shard_map/ppermute | solution.py:17
  337.0 2.0 copy-done.6
  339.0 6.1 %collective-permute-done.3 = f32[64,16384]{1,0:T(8,128)} collective-permute-done((f32[64,16384]{1,0:T(8,128)S(1)}, f32[64,16384]{1,0:T(8,128)}, u32[]{:S(2)}, u32[]{:S(2)}) %collective-permute-start.3) | collective-permute-done | bytes 4194336 | tf_op jit(solution)/shard_map/ppermute | solution.py:17
  345.1 6.2 %slice_select_fusion.4 = (f32[64,16384]{1,0:T(8,128)S(1)}, f32[64,16384]{1,0:T(8,128)}) fusion(f32[64,16384]{1,0:T(8,128)} %copy-done.6, f32[128,16384]{1,0:T(8,128)S(1)} %fusion.8, pred[]{:T(512)S(6)} %eq.1664, f32[64,16384]{1,0:T(8,128)} %collective-permute-done.3, pred[]{:T(512)S(6)} %eq.1694), kind=kLoop, calls=%fused_computation.18 | loop fusion | flops 2097152 | bytes 20971522 | tf_op jit(solution)/shard_map/jit(_where)/select_n | solution.py:80
  351.3 10.2 %fusion.168 = (f32[128]{0:T(128)S(1)}, f32[128]{0:T(128)S(1)}, f32[128]{0:T(128)S(1)}, f32[128,128]{0,1:T(8,128)S(1)}) fusion(s32[128]{0:T(128)S(1)} %iota_xor_fusion.6, f32[64,16384]{1,0:T(8,128)} %get-tuple-element.170, f32[64,16384]{1,0:T(8,128)S(1)} %get-tuple-element.169), kind=kOutput, calls=%fused_computation.281 | convolution fusion | flops 3223436800 | bytes 8456192 | tf_op jit(solution)/shard_map/in,jn->ij/dot_general | solution.py:83
  371.9 9.2 %fusion.6 = f32[128,16384]{1,0:T(8,128)S(1)} fusion(f32[128,128]{1,0:T(8,128)S(1)} %fusion.48, f32[64,16384]{1,0:T(8,128)} %get-tuple-element.170, f32[64,16384]{1,0:T(8,128)S(1)} %get-tuple-element.169), kind=kOutput, calls=%fused_computation.10 | convolution fusion | flops 3223322624 | bytes 16842752 | tf_op jit(solution)/shard_map/in,ij->jn/dot_general | solution.py:86
  383.7 2.6 collective-permute-start.5
  386.3 42.8 %collective-permute-done.4 = f32[64,16384]{1,0:T(8,128)S(1)} collective-permute-done((f32[64,16384]{1,0:T(8,128)S(1)}, f32[64,16384]{1,0:T(8,128)S(1)}, u32[]{:S(2)}, u32[]{:S(2)}) %collective-permute-start.4) | collective-permute-done | bytes 4194336 | tf_op jit(solution)/shard_map/ppermute | solution.py:17
  429.1 2.0 copy-done.5
  431.2 6.1 %collective-permute-done.5 = f32[64,16384]{1,0:T(8,128)} collective-permute-done((f32[64,16384]{1,0:T(8,128)S(1)}, f32[64,16384]{1,0:T(8,128)}, u32[]{:S(2)}, u32[]{:S(2)}) %collective-permute-start.5) | collective-permute-done | bytes 4194336 | tf_op jit(solution)/shard_map/ppermute | solution.py:17
  437.3 6.2 %slice_select_fusion.1 = (f32[64,16384]{1,0:T(8,128)S(1)}, f32[64,16384]{1,0:T(8,128)}) fusion(f32[64,16384]{1,0:T(8,128)} %copy-done.5, f32[128,16384]{1,0:T(8,128)S(1)} %fusion.6, pred[]{:T(512)S(6)} %eq.1664, f32[64,16384]{1,0:T(8,128)} %collective-permute-done.5, pred[]{:T(512)S(6)} %eq.1694), kind=kLoop, calls=%fused_computation.15 | loop fusion | flops 2097152 | bytes 20971522 | tf_op jit(solution)/shard_map/jit(_where)/select_n | solution.py:80
  443.4 10.3 %fusion.172 = (f32[128]{0:T(128)S(1)}, f32[128]{0:T(128)S(1)}, f32[128]{0:T(128)S(1)}, f32[128,128]{0,1:T(8,128)S(1)}) fusion(s32[128]{0:T(128)S(1)} %iota_xor_fusion.6, f32[64,16384]{1,0:T(8,128)} %get-tuple-element.166, f32[64,16384]{1,0:T(8,128)S(1)} %get-tuple-element.165), kind=kOutput, calls=%fused_computation.285 | convolution fusion | flops 3223436800 | bytes 8456192 | tf_op jit(solution)/shard_map/in,jn->ij/dot_general | solution.py:83
  464.0 15.4 %fusion.4 = f32[16384,128]{1,0:T(8,128)} fusion(f32[128,128]{1,0:T(8,128)S(1)} %fusion.23, f32[64,16384]{1,0:T(8,128)S(1)} %copy-done.1, f32[64,16384]{1,0:T(8,128)S(1)} %get-tuple-element.165), kind=kOutput, calls=%fused_computation.8 | convolution fusion | flops 3223322624 | bytes 16842752 | tf_op jit(solution)/shard_map/in,ij->nj/dot_general | solution.py:88
  (209 shorter events, 53.5 us)
Async XLA Ops:
  9.3 10.0 %copy-start.3 = (f32[16,128,8,128]{1,3,0,2:T(8,128)S(1)}, f32[16,128,8,128]{1,3,0,2:T(8,128)}, u32[]{:S(2)}) copy-start(f32[16,128,8,128]{1,3,0,2:T(8,128)} %copy.21) | copy-start | bytes 25165828
  23.6 120.5 %all-to-all-start = ((f32[8,16,1,128,1,128]{3,5,1,4,2,0:T(8,128)}), f32[8,16,1,128,1,128]{3,5,1,4,2,0:T(8,128)}, u32[]{:S(2)}, u32[]{:S(2)}) async-start(f32[8,16,1,128,1,128]{3,5,1,4,2,0:T(8,128)} %fusion.15), calls=%async_computation | async-start | bytes 16777216 | tf_op jit(solution)/shard_map/all_to_all | solution.py:61
  161.3 20.9 %copy-start.4 = (f32[16,8,1,128,1,128]{5,3,1,0,4,2:T(8,128)S(1)}, f32[16,8,1,128,1,128]{5,3,1,0,4,2:T(8,128)}, u32[]{:S(2)}) copy-start(f32[16,8,1,128,1,128]{5,3,1,0,4,2:T(8,128)} %copy.24) | copy-start | bytes 25165828
  191.4 5.9 %copy-start = (f32[128,16384]{1,0:T(8,128)}, f32[128,16384]{1,0:T(8,128)S(1)}, u32[]{:S(2)}) copy-start(f32[128,16384]{1,0:T(8,128)S(1)} %fusion.830) | copy-start | bytes 25165828
  197.4 52.1 %collective-permute-start = (f32[64,16384]{1,0:T(8,128)}, f32[64,16384]{1,0:T(8,128)}, u32[]{:S(2)}, u32[]{:S(2)}) collective-permute-start(f32[64,16384]{1,0:T(8,128)} %get-tuple-element.175), channel_id=1, source_target_pairs={{0,1},{1,2},{2,3},{3,4},{4,5},{5,6},{6,7},{7,8},{8,9},{9,10},{10,1... | collective-permute-start | bytes 12582920 | tf_op jit(solution)/shard_map/ppermute | solution.py:17
  203.7 53.8 %collective-permute-start.1 = (f32[64,16384]{1,0:T(8,128)}, f32[64,16384]{1,0:T(8,128)}, u32[]{:S(2)}, u32[]{:S(2)}) collective-permute-start(f32[64,16384]{1,0:T(8,128)} %get-tuple-element.176), channel_id=1, source_target_pairs={{1,0},{2,1},{3,2},{4,3},{5,4},{6,5},{7,6},{8,7},{9,8},{10,9},{11,1... | collective-permute-start | bytes 12582920 | tf_op jit(solution)/shard_map/ppermute | solution.py:17
  262.8 16.6 %copy-start.2 = (f32[64,16384]{1,0:T(8,128)}, f32[64,16384]{1,0:T(8,128)S(1)}, u32[]{:S(2)}) copy-start(f32[64,16384]{1,0:T(8,128)S(1)} %get-tuple-element.174) | copy-start | bytes 12582916
  289.6 47.4 %collective-permute-start.2 = (f32[64,16384]{1,0:T(8,128)S(1)}, f32[64,16384]{1,0:T(8,128)S(1)}, u32[]{:S(2)}, u32[]{:S(2)}) collective-permute-start(f32[64,16384]{1,0:T(8,128)S(1)} %get-tuple-element.171), channel_id=1, source_target_pairs={{0,1},{1,2},{2,3},{3,4},{4,5},{5,6},{6,7},{7,8},{8,9},{9,10},{10,1... | collective-permute-start | bytes 12582920 | tf_op jit(solution)/shard_map/ppermute | solution.py:17
  291.6 53.5 %collective-permute-start.3 = (f32[64,16384]{1,0:T(8,128)S(1)}, f32[64,16384]{1,0:T(8,128)}, u32[]{:S(2)}, u32[]{:S(2)}) collective-permute-start(f32[64,16384]{1,0:T(8,128)S(1)} %get-tuple-element.172), channel_id=1, source_target_pairs={{1,0},{2,1},{3,2},{4,3},{5,4},{6,5},{7,6},{8,7},{9,8},{10,9},{11,1... | collective-permute-start | bytes 12582920 | tf_op jit(solution)/shard_map/ppermute | solution.py:17
  337.0 2.0 copy-start.6
  381.8 47.4 %collective-permute-start.4 = (f32[64,16384]{1,0:T(8,128)S(1)}, f32[64,16384]{1,0:T(8,128)S(1)}, u32[]{:S(2)}, u32[]{:S(2)}) collective-permute-start(f32[64,16384]{1,0:T(8,128)S(1)} %get-tuple-element.167), channel_id=1, source_target_pairs={{0,1},{1,2},{2,3},{3,4},{4,5},{5,6},{6,7},{7,8},{8,9},{9,10},{10,1... | collective-permute-start | bytes 12582920 | tf_op jit(solution)/shard_map/ppermute | solution.py:17
  383.7 53.5 %collective-permute-start.5 = (f32[64,16384]{1,0:T(8,128)S(1)}, f32[64,16384]{1,0:T(8,128)}, u32[]{:S(2)}, u32[]{:S(2)}) collective-permute-start(f32[64,16384]{1,0:T(8,128)S(1)} %get-tuple-element.168), channel_id=1, source_target_pairs={{1,0},{2,1},{3,2},{4,3},{5,4},{6,5},{7,6},{8,7},{9,8},{10,9},{11,1... | collective-permute-start | bytes 12582920 | tf_op jit(solution)/shard_map/ppermute | solution.py:17
  429.1 2.0 copy-start.5
  443.4 20.5 %copy-start.1 = (f32[64,16384]{1,0:T(8,128)S(1)}, f32[64,16384]{1,0:T(8,128)}, u32[]{:S(2)}) copy-start(f32[64,16384]{1,0:T(8,128)} %get-tuple-element.166) | copy-start | bytes 12582916
